TPU v7x, 128 devices: a whole 4x4x4 slice. The times are simulated.
128 devices in a mesh: blk: 32 (over z, x, core), nb: 4 (over y).
Axes of the slice: x: 4, y: 4, z: 4, core: 2. Of those that a mesh axis runs over, the one named last changes fastest.
Arguments:
- latent: float32 [1024, 96, 128], P(('blk', 'nb')), may hold values from -8 to 8
- coords: float32 [1024, 2, 128], P(('blk', 'nb')), may hold values from 0 to 1
- labels: int32 [1024, 96, 128], P(('blk', 'nb')), may hold values 0 or 1
- owner: int32 [1024, 4], P(('blk', 'nb')), may hold values from 0 to 127, all different within a row; in each aligned block of 8 rows (0 to 7, 8 to 15, ...) at most 2 rows name the same one
- slot: int32 [1024, 4], P(('blk', 'nb')), may hold values from 0 to 7
Outputs:
- new_latent: float32 [1024, 96, 128], P(('blk', 'nb'))
- step_rms: float32 [96], replicated
Inputs may be any that keep to these rules, and one draw needn't show every extreme that they name: The 4 owners of one block are distinct; the 8 blocks stored on one device name any one owner at most 2 times.
All inputs are finite; a program needn't handle non-finite values. No bound on the sum of `labels` on one device may be relied on, other than what follows from the above.
Results may differ from a plain program's by a relative error of at most 0.0003.
Values sent between devices are 32-bit elements; how exact they have to be, the bound alone decides.
A program may use at most 192 MiB of HBM per device.

v0:
```python
import math

import jax
import jax.numpy as jnp
from jax import lax
from jax.sharding import PartitionSpec as P

nugget = 0.25
length_scale = 0.1


def covariance(points):
    east_gap = points[:, 0, :, None] - points[:, 0, None, :]
    north_gap = points[:, 1, :, None] - points[:, 1, None, :]
    scaled = jnp.sqrt(east_gap * east_gap + north_gap * north_gap) * (math.sqrt(3.0) / length_scale)
    kernel = (1.0 + scaled) * jnp.exp(-scaled)
    matrix_order = points.shape[-1]
    return kernel + nugget * jnp.eye(matrix_order, dtype=jnp.float32)


def factor_group(bundle):
    points, values = bundle
    factor = jnp.linalg.cholesky(covariance(points))
    width = values.shape[-1]
    own_width = width // 5
    split = width - own_width
    whitened = lax.linalg.triangular_solve(
        factor, values, left_side=False, lower=True, transpose_a=True
    )
    target = jnp.concatenate(
        [jnp.zeros_like(whitened[..., :split]), whitened[..., split:]], axis=-1
    )
    pulled = lax.linalg.triangular_solve(
        factor, target, left_side=False, lower=True, transpose_a=False
    )
    corner = factor[:, split:, split:]
    identity = jnp.broadcast_to(jnp.eye(own_width, dtype=jnp.float32), corner.shape)
    inverse = lax.linalg.triangular_solve(corner, identity, left_side=True, lower=True)
    return (pulled, jnp.sum(inverse * inverse, axis=-2))


def probit_ratio(margin):
    density = jnp.exp(-0.5 * margin * margin - 0.5 * math.log(2.0 * math.pi))
    mass = 0.5 * lax.erfc(-margin / math.sqrt(2.0))
    return density / mass


def body(latent, coords, labels, owner, slot):
    block_count = latent.shape[0]
    field_count = latent.shape[1]
    point_count = latent.shape[2]
    near_count = owner.shape[1]
    blk_count = lax.axis_size("blk")
    part_count = lax.axis_size("nb")
    device_count = blk_count * part_count
    capacity = max(2, 2 * block_count * near_count // device_count)
    wanted = owner.reshape(-1)
    places = slot.reshape(-1)
    request_count = wanted.shape[0]
    earlier = lax.broadcasted_iota(
        jnp.int32, (request_count, request_count), 1
    ) < lax.broadcasted_iota(jnp.int32, (request_count, request_count), 0)
    slot_rank = jnp.sum(
        jnp.where((wanted[None, :] == wanted[:, None]) & earlier, 1, 0), axis=1
    ).astype(jnp.int32)
    position = wanted * capacity + slot_rank
    requests = jnp.full((device_count * capacity,), -1, jnp.int32).at[position].set(places)
    payload = jnp.concatenate([latent, coords], axis=1)
    received = lax.all_to_all(
        requests.reshape(device_count, capacity),
        ("blk", "nb"),
        split_axis=0,
        concat_axis=0,
        tiled=True,
    )
    live = received >= 0
    picked = payload[jnp.maximum(received, 0)]
    picked = jnp.where(live[..., None, None], picked, 0.0)
    picked, kept = (picked, received)
    fetched = lax.all_to_all(picked, ("blk", "nb"), split_axis=0, concat_axis=0, tiled=True)
    arrived = fetched.reshape(device_count * capacity, field_count + 2, point_count)[position]
    arrived = arrived.reshape(block_count, near_count, field_count + 2, point_count)
    near_values = (
        arrived[:, :, :field_count, :]
        .transpose(0, 2, 1, 3)
        .reshape(block_count, field_count, near_count * point_count)
    )
    near_points = (
        arrived[:, :, field_count:, :]
        .transpose(0, 2, 1, 3)
        .reshape(block_count, 2, near_count * point_count)
    )
    values = jnp.concatenate([near_values, latent], axis=-1)
    points = jnp.concatenate([near_points, coords], axis=-1)
    per_step = math.gcd(block_count, 8)
    width = (near_count + 1) * point_count
    pulled, qdiag = lax.map(
        factor_group,
        (
            points.reshape(block_count // per_step, per_step, 2, width),
            values.reshape(block_count // per_step, per_step, field_count, width),
        ),
    )
    pulled = pulled.reshape(block_count, field_count, width)
    qdiag = qdiag.reshape(block_count, point_count)
    split = near_count * point_count
    parts = (
        pulled[..., :split]
        .reshape(block_count, field_count, near_count, point_count)
        .transpose(0, 2, 1, 3)
    )
    outgoing = (
        jnp.zeros((device_count * capacity, field_count, point_count), jnp.float32)
        .at[position]
        .set(parts.reshape(request_count, field_count, point_count))
    )
    returned = lax.all_to_all(
        outgoing.reshape(device_count, capacity, field_count, point_count),
        ("blk", "nb"),
        split_axis=0,
        concat_axis=0,
        tiled=True,
    )
    asked_flat = kept.reshape(-1)
    selector = (asked_flat[None, :] == lax.broadcasted_iota(jnp.int32, (block_count, 1), 0)).astype(
        jnp.float32
    )
    summed = jnp.dot(
        selector,
        returned.reshape(device_count * capacity, field_count * point_count),
        precision=lax.Precision.HIGHEST,
        preferred_element_type=jnp.float32,
    )
    prior = summed.reshape(block_count, field_count, point_count) + pulled[..., split:]
    sign = 2.0 * labels.astype(jnp.float32) - 1.0
    margin = sign * latent
    ratio = probit_ratio(margin)
    weight = ratio * (ratio + margin)
    delta = (sign * ratio - prior) / (weight + qdiag[:, None, :])
    spread = lax.psum(jnp.sum(delta * delta, axis=(0, 2)), ("blk", "nb"))
    step_rms = jnp.sqrt(spread / (block_count * point_count * device_count) + 1e-06)
    new_latent = latent + 0.5 * delta / step_rms[None, :, None]
    return (new_latent, step_rms)


def solution(mesh):
    return jax.shard_map(
        body,
        mesh=mesh,
        in_specs=(
            P(("blk", "nb"), None, None),
            P(("blk", "nb"), None, None),
            P(("blk", "nb"), None, None),
            P(("blk", "nb"), None),
            P(("blk", "nb"), None),
        ),
        out_specs=(P(("blk", "nb"), None, None), P()),
        check_vma=False,
    )
```

profile of v0, /device:TPU:1, one launch (start us, length us, event | category | flops | bytes accessed | tf_op | source)
XLA Modules:
  0.0 1848.8 jit_solution(16784902397886408551)
XLA Ops:
  4.8 11.5 all-to-all-start
  17.4 8.5 all-to-all-done
  28.2 6.3 gather_fusion
  34.5 12.0 copy.187
  46.9 9.3 broadcast_select_fusion
  56.2 5.8 copy.188
  62.0 5.9 all-to-all-start.1
  71.1 157.7 %all-to-all-done.1 = f32[128,2,98,128]{3,1,2,0:T(2,128)} async-done(((f32[128,2,98,128]{3,1,2,0:T(2,128)}), f32[128,2,98,128]{3,1,2,0:T(2,128)}, u32[]{:S(2)}, u32[]{:S(2)}) %all-to-all-start.1) | async-done | bytes 12845088 | tf_op jit(solution)/shard_map/all_to_all | solution.py:80
  228.8 10.8 copy.189
  247.5 18.4 add_multiply_fusion
  270.5 93.8 %custom-call.59 = f32[8,128,128]{2,1,0:T(8,128)S(1)} custom-call(f32[8,128,128]{2,1,0:T(8,128)S(1)} %cholesky.364), custom_call_target="Cholesky" | custom-call | tf_op jit(solution)/shard_map/while/body/eval_jaxpr/jit(cholesky)/cholesky | solution.py:23
  364.4 79.1 %custom-call.60 = f32[8,1,128,128]{2,3,1,0:T(8,128)S(1)} custom-call(f32[8,1,128,128]{3,2,1,0:T(8,128)S(1)} %select_bitcast_fusion.3), custom_call_target="InvertDiagBlocksLowerTriangular" | custom-call | tf_op jit(solution)/shard_map/while/body/eval_jaxpr/jit(cholesky)/cholesky | solution.py:23
  443.5 5.8 cholesky.306
  458.6 94.6 %custom-call.61 = f32[8,128,128]{2,1,0:T(8,128)S(1)} custom-call(f32[8,128,128]{2,1,0:T(8,128)} %cholesky.368), custom_call_target="Cholesky" | custom-call | tf_op jit(solution)/shard_map/while/body/eval_jaxpr/jit(cholesky)/cholesky | solution.py:23
  555.0 80.2 %custom-call.62 = f32[8,1,128,128]{2,3,1,0:T(8,128)} custom-call(f32[8,1,128,128]{3,2,1,0:T(8,128)} %get-tuple-element.55), custom_call_target="InvertDiagBlocksLowerTriangular" | custom-call | tf_op jit(solution)/shard_map/while/body/eval_jaxpr/jit(cholesky)/cholesky | solution.py:23
  639.0 5.6 slice_subtract_fusion.1
  645.4 94.6 %custom-call.63 = f32[8,128,128]{2,1,0:T(8,128)S(1)} custom-call(f32[8,128,128]{2,1,0:T(8,128)} %cholesky.373), custom_call_target="Cholesky" | custom-call | tf_op jit(solution)/shard_map/while/body/eval_jaxpr/jit(cholesky)/cholesky | solution.py:23
  741.9 80.2 %custom-call.64 = f32[8,1,128,128]{2,3,1,0:T(8,128)} custom-call(f32[8,1,128,128]{3,2,1,0:T(8,128)} %get-tuple-element.53), custom_call_target="InvertDiagBlocksLowerTriangular" | custom-call | tf_op jit(solution)/shard_map/while/body/eval_jaxpr/jit(cholesky)/cholesky | solution.py:23
  825.2 5.6 fusion.36
  831.7 94.6 %custom-call.65 = f32[8,128,128]{2,1,0:T(8,128)S(1)} custom-call(f32[8,128,128]{2,1,0:T(8,128)} %cholesky.378), custom_call_target="Cholesky" | custom-call | tf_op jit(solution)/shard_map/while/body/eval_jaxpr/jit(cholesky)/cholesky | solution.py:23
  928.1 80.4 %custom-call.66 = f32[8,1,128,128]{2,3,1,0:T(8,128)} custom-call(f32[8,1,128,128]{3,2,1,0:T(8,128)} %get-tuple-element.51), custom_call_target="InvertDiagBlocksLowerTriangular" | custom-call | tf_op jit(solution)/shard_map/while/body/eval_jaxpr/jit(cholesky)/cholesky | solution.py:23
  1015.4 93.8 %custom-call.67 = f32[8,128,128]{2,1,0:T(8,128)S(1)} custom-call(f32[8,128,128]{2,1,0:T(8,128)S(1)} %fusion.41), custom_call_target="Cholesky" | custom-call | tf_op jit(solution)/shard_map/while/body/eval_jaxpr/jit(cholesky)/cholesky | solution.py:23
  1111.6 12.5 broadcast_select_fusion.1
  1124.1 20.8 %while.1 = (s32[]{:T(128)}, f32[8,640,640]{2,1,0:T(8,128)}, s32[5,2]{0,1:T(2,128)S(1)}, f32[5,8,128,128]{3,2,0,1:T(8,128)}, s32[]{:T(128)}) while((s32[]{:T(128)}, f32[8,640,640]{2,1,0:T(8,128)}, s32[5,2]{0,1:T(2,128)S(1)}, f32[5,8,128,128]{3,2,0,1:T(8,128)}, s32[]{:T(128)}) %tuple.42), condition=%wide.while_cond, body=%wide.while_body.sunk | while | flops 2 | bytes 1050209 | solution.py:27
  1144.9 393.7 %custom-call.68 = f32[8,5,128,128]{2,3,1,0:T(8,128)S(1)} custom-call(f32[8,5,128,128]{3,2,1,0:T(8,128)} %bitcast.127), custom_call_target="InvertDiagBlocksLowerTriangular" | custom-call | tf_op jit(solution)/shard_map/while/body/eval_jaxpr/triangular_solve | solution.py:27
  1568.6 6.2 broadcast_in_dim.54
  1586.1 79.0 %custom-call.69 = f32[8,1,128,128]{2,3,1,0:T(8,128)S(1)} custom-call(f32[8,1,128,128]{3,2,1,0:T(8,128)S(1)} %fusion.81), custom_call_target="InvertDiagBlocksLowerTriangular" | custom-call | tf_op jit(solution)/shard_map/while/body/eval_jaxpr/triangular_solve | solution.py:38
  1666.1 74.3 %all-to-all-done.2 = f32[128,2,96,128]{3,2,1,0:T(8,128)} async-done(((f32[128,2,96,128]{3,2,1,0:T(8,128)}), f32[128,2,96,128]{3,2,1,0:T(8,128)}, u32[]{:S(2)}, u32[]{:S(2)}) %all-to-all-start.2) | async-done | bytes 12582944 | tf_op jit(solution)/shard_map/all_to_all | solution.py:117
  1740.5 20.6 %copy.259 = f32[32,8,96,128]{3,1,2,0:T(8,128)} copy(f32[32,8,96,128]{3,2,1,0:T(8,128)} %bitcast.48) | data formatting | bytes 25165824
  1761.1 12.6 copy.212
  1773.7 8.6 fusion.124
  1783.6 64.1 %psum.7 = f32[96]{0:T(128)S(1)} all-reduce(f32[96]{0:T(128)S(1)} %get-tuple-element.40), channel_id=1, replica_groups=mesh['blk'=32,'nb'=4] {'blk','nb'}, use_global_device_ids=true, to_apply=%region_15.16 | all-reduce | flops 96 | bytes 768 | tf_op jit(solution)/shard_map/psum | solution.py:140
  (127 shorter events, 121.3 us)
Async XLA Ops:
  3.3 65.1 %copy-start.9 = (s32[32]{0:T(128)}, s32[32]{0:T(128)S(1)}, u32[]{:S(2)}) copy-start(s32[32]{0:T(128)S(1)} %fusion.127) | copy-start | bytes 388
  4.8 21.1 %all-to-all-start = ((s32[128,1,2]{2,1,0:T(1,128)}), s32[128,1,2]{2,1,0:T(1,128)S(1)}, u32[]{:S(2)}, u32[]{:S(2)}) async-start(s32[128,1,2]{2,1,0:T(1,128)} %bitcast.2), calls=%async_computation | async-start | bytes 131072 | tf_op jit(solution)/shard_map/all_to_all | solution.py:69
  62.0 166.8 %all-to-all-start.1 = ((f32[128,2,98,128]{3,1,2,0:T(2,128)}), f32[128,2,98,128]{3,1,2,0:T(2,128)}, u32[]{:S(2)}, u32[]{:S(2)}) async-start(f32[128,2,98,128]{3,1,2,0:T(2,128)} %copy.188), calls=%async_computation.1 | async-start | bytes 25690112 | tf_op jit(solution)/shard_map/all_to_all | solution.py:80
  68.4 295.9 %copy-start.4 = (pred[128,128]{1,0:T(8,128)(4,1)}, pred[128,128]{1,0:T(8,128)(4,1)S(1)}, u32[]{:S(2)}) copy-start(pred[128,128]{1,0:T(8,128)(4,1)S(1)} %iota_compare_fusion.3) | copy-start | bytes 49156
  245.1 1.7 copy-start.8
  245.5 2.0 copy-start.3
  265.8 4.7 copy-start.2
  1111.6 12.5 copy-start.12
  1538.6 15.8 copy-start.1
  1543.1 11.3 copy-start
  1568.6 6.2 copy-start.10
  1579.8 5.0 copy-start.7
  1579.8 5.2 copy-start.5
  1579.8 160.7 %all-to-all-start.2 = ((f32[128,2,96,128]{3,2,1,0:T(8,128)}), f32[128,2,96,128]{3,2,1,0:T(8,128)}, u32[]{:S(2)}, u32[]{:S(2)}) async-start(f32[128,2,96,128]{3,2,1,0:T(8,128)} %bitcast.118), calls=%async_computation.2 | async-start | bytes 25165824 | tf_op jit(solution)/shard_map/all_to_all | solution.py:117
  1773.7 8.6 copy-start.6
  1847.7 0.9 copy-start.11
where the time goes:
time: 1860 us; the launch traced here: 1850 us
  other arithmetic  1320 us (71%)
  waiting for transfers between devices  241 us (13%)
  local copies, waits for them, and re-layouts  130 us (7%)
  matrix products  68.2 us (4%)
  blocking collectives  64.1 us (3%)
  starting transfers between devices  22.3 us (1%)
    another operation x22, other arithmetic, factor_group(): factor = jnp.linalg.cholesky(covariance(points))  800 us
    another operation x4, other arithmetic, factor_group(): lax.linalg.triangular_solve(factor, values, left_side=False, lower=True,...  407 us
    all_to_all x1, waiting for transfers between devices, body(): lax.all_to_all(picked, ('blk', 'nb'), split_axis=0, concat_axis=0, tiled=...  158 us
    another operation x2, other arithmetic, factor_group(): lax.linalg.triangular_solve(corner, identity, left_side=True, lower=True)  80.1 us
    all_to_all x1, waiting for transfers between devices, body(): lax.all_to_all(outgoing.reshape(device_count, capacity, field_count, poin...  74.3 us
    psum x1, blocking collectives, body(): spread = lax.psum(jnp.sum(delta * delta, axis=(0, 2)), ('blk', 'nb'))  64.1 us
  transfers between devices with their start and end apart: 3, of which 3 were waited for; matrix products, arithmetic and copies ran while one was open for 5% of the time, Pallas kernels for 0%

commit v1 on v0

v1 whole, which is shorter than its diff:
```python
import math
import functools
import jax
import jax.numpy as jnp
from jax import lax
from jax.experimental import pallas as pl
from jax.experimental.pallas import tpu as pltpu
from jax.sharding import PartitionSpec as P

nugget = 0.25
length_scale = 0.1
HI = lax.Precision.HIGHEST
NN = (((1,), (0,)), ((), ()))
NT = (((1,), (1,)), ((), ()))
TN = (((0,), (0,)), ((), ()))


def dot(a, b, dims=NN):
    return lax.dot_general(a, b, dims, precision=HI, preferred_element_type=jnp.float32)


def sweep64(pack):
    lane = lax.broadcasted_iota(jnp.int32, (64, 128), 1)
    base = lane & 64
    inner = lane & 63

    def step(t, carry):
        p = 2 * t
        at0 = base + p
        at1 = at0 + 1
        own = (inner == p) | (inner == p + 1)
        for q in range(4):
            rows = pack[q, pl.ds(p, 2), :]
            r1 = jnp.broadcast_to(rows[0:1], (8, 128))
            r2 = jnp.broadcast_to(rows[1:2], (8, 128))
            a = jnp.take_along_axis(r1, at0[:8], axis=1)
            b = jnp.take_along_axis(r1, at1[:8], axis=1)
            d = jnp.take_along_axis(r2, at1[:8], axis=1)
            rdet = 1.0 / (a * d - b * b)
            first = inner[:8] == p
            second = inner[:8] == p + 1
            r1 = jnp.where(first, 1.0, jnp.where(second, 0.0, r1))
            r2 = jnp.where(first, 0.0, jnp.where(second, 1.0, r2))
            new1 = (d * r1 - b * r2) * rdet
            new2 = (a * r2 - b * r1) * rdet
            for s in range(8):
                x = pack[q, pl.ds(8 * s, 8), :]
                c1 = jnp.take_along_axis(x, at0[:8], axis=1)
                c2 = jnp.take_along_axis(x, at1[:8], axis=1)
                x = jnp.where(own[:8], 0.0, x)
                pack[q, pl.ds(8 * s, 8), :] = x - c1 * new1 - c2 * new2
            pack[q, pl.ds(p, 2), :] = jnp.concatenate([new1[0:1], new2[0:1]], axis=0)
        return carry

    lax.fori_loop(0, 32, step, 0)


def factor_kernel(nbr_ref, self_ref, coords_ref, own_ref, gt_ref, si_ref, cov, upper, tile, dinv, pack):
    n = own_ref.shape[0]
    near = nbr_ref.shape[1]
    nt = near + 1
    scale = math.sqrt(3.0) / length_scale

    def build(m, carry):
        pts = [coords_ref[nbr_ref[m, k]] for k in range(near)] + [own_ref[m]]
        for i in range(nt):
            xc = jnp.broadcast_to(pts[i][0:1], (128, 128)).T
            yc = jnp.broadcast_to(pts[i][1:2], (128, 128)).T
            for j in range(i + 1):
                dx = xc - pts[j][0:1]
                dy = yc - pts[j][1:2]
                s = jnp.sqrt(dx * dx + dy * dy) * scale
                c = (1.0 + s) * jnp.exp(-s)
                if i == j:
                    r = lax.broadcasted_iota(jnp.int32, (128, 128), 0)
                    q = lax.broadcasted_iota(jnp.int32, (128, 128), 1)
                    c = c + jnp.where(r == q, nugget, 0.0)
                cov[m, i * 128:(i + 1) * 128, j * 128:(j + 1) * 128] = c
        return carry

    lax.fori_loop(0, n, build, 0)

    for j in range(nt):
        lo, hi = j * 128, (j + 1) * 128

        def left(m, carry):
            p = cov[m, lo:, lo:hi]
            if j:
                p = p - dot(upper[m, lo:, :lo], tile[m, lo:hi, :lo], NT)
            tile[m, lo:, lo:hi] = p
            return carry

        lax.fori_loop(0, n, left, 0)

        for q in range(n // 2):
            pack[q] = jnp.concatenate(
                [tile[2 * q, lo:lo + 64, lo:lo + 64], tile[2 * q + 1, lo:lo + 64, lo:lo + 64]], axis=1
            )
        sweep64(pack)
        for m in range(n):
            at = (m % 2) * 64
            ai = pack[m // 2, :, at:at + 64]
            b = tile[m, lo + 64:hi, lo:lo + 64]
            v = dot(b, ai)
            dinv[m, 0:64, 0:64] = ai
            dinv[m, 64:128, 0:64] = v
            dinv[m, 64:128, 64:128] = tile[m, lo + 64:hi, lo + 64:hi] - dot(v, b, NT)
        for q in range(n // 2):
            pack[q] = jnp.concatenate(
                [dinv[2 * q, 64:128, 64:128], dinv[2 * q + 1, 64:128, 64:128]], axis=1
            )
        sweep64(pack)
        for m in range(n):
            at = (m % 2) * 64
            si = pack[m // 2, :, at:at + 64]
            v = dinv[m, 64:128, 0:64]
            w = dot(si, v)
            dinv[m, 64:128, 64:128] = si
            dinv[m, 64:128, 0:64] = -w
            dinv[m, 0:64, 64:128] = -w.T
            dinv[m, 0:64, 0:64] = dinv[m, 0:64, 0:64] + dot(v, w, TN)

        if j < nt - 1:
            def scale_panel(m, carry):
                upper[m, hi:, lo:hi] = dot(tile[m, hi:, lo:hi], dinv[m])
                return carry

            lax.fori_loop(0, n, scale_panel, 0)

    def back(m, carry):
        last = near * 128
        si_ref[m] = dinv[m]
        for k in reversed(range(near)):
            g = upper[m, last:, k * 128:(k + 1) * 128]
            if k < near - 1:
                g = g - dot(gt_ref[m, :, (k + 1) * 128:last], upper[m, (k + 1) * 128:last, k * 128:(k + 1) * 128])
            gt_ref[m, :, k * 128:(k + 1) * 128] = g
        return carry

    lax.fori_loop(0, n, back, 0)


def factor(nbr, coords_all, coords_own):
    n, near = nbr.shape
    width = (near + 1) * 128
    return pl.pallas_call(
        factor_kernel,
        out_shape=(
            jax.ShapeDtypeStruct((n, 128, near * 128), jnp.float32),
            jax.ShapeDtypeStruct((n, 128, 128), jnp.float32),
        ),
        in_specs=[pl.BlockSpec(memory_space=pltpu.SMEM), pl.BlockSpec(memory_space=pltpu.SMEM)]
        + [pl.BlockSpec(memory_space=pltpu.VMEM)] * 2,
        out_specs=(pl.BlockSpec(memory_space=pltpu.VMEM),) * 2,
        scratch_shapes=[
            pltpu.VMEM((n, width, width), jnp.float32),
            pltpu.VMEM((n, width, width - 128), jnp.float32),
            pltpu.VMEM((n, width, width), jnp.float32),
            pltpu.VMEM((n, 128, 128), jnp.float32),
            pltpu.VMEM((n // 2, 64, 128), jnp.float32),
        ],
        compiler_params=pltpu.CompilerParams(vmem_limit_bytes=56 * 1024 * 1024),
        cost_estimate=pl.CostEstimate(flops=2_000_000_000, bytes_accessed=5_000_000, transcendentals=4_000_000),
        name="factor",
    )(nbr, nbr, coords_all, coords_own)


def apply_kernel(nbr_ref, pos_ref, v0_ref, v1_ref, v2_ref, v3_ref, own_ref, gt_ref, si_ref, zero_ref, out_ref, u_ref, keep):
    k = pl.program_id(1)

    @pl.when(k == 0)
    def _():
        r = own_ref[0]
        for i, v in enumerate((v0_ref, v1_ref, v2_ref, v3_ref)):
            r = r - dot(v[0], gt_ref[0, :, i * 128:(i + 1) * 128], NT)
        u = dot(r, si_ref[0])
        keep[...] = u
        u_ref[0] = u

    g = gt_ref[0, :, pl.ds(pl.multiple_of(k * 128, 128), 128)]
    out_ref[0] = -dot(keep[...], g)


def apply_blocks(nbr, pos, latent_all, latent, gt, si, zero):
    n, near = nbr.shape
    fields = latent.shape[1]
    def v_spec(i):
        return pl.BlockSpec((1, fields, 128), lambda b, k, nbr, pos: (nbr[b * near + i], 0, 0))
    def b_spec(*shape):
        return pl.BlockSpec((1,) + shape, lambda b, k, nbr, pos: (b, 0, 0))
    return pl.pallas_call(
        apply_kernel,
        out_shape=(
            jax.ShapeDtypeStruct(zero.shape, jnp.float32),
            jax.ShapeDtypeStruct(latent.shape, jnp.float32),
        ),
        grid_spec=pltpu.PrefetchScalarGridSpec(
            num_scalar_prefetch=2,
            grid=(n, near),
            in_specs=[v_spec(i) for i in range(near)]
            + [b_spec(fields, 128), b_spec(128, near * 128), b_spec(128, 128), pl.BlockSpec(memory_space=pl.ANY)],
            out_specs=(
                pl.BlockSpec((1, fields, 128), lambda b, k, nbr, pos: (pos[b * near + k], 0, 0)),
                b_spec(fields, 128),
            ),
            scratch_shapes=[pltpu.VMEM((fields, 128), jnp.float32)],
        ),
        input_output_aliases={9: 0},
        name="apply",
    )(nbr.reshape(-1), pos.reshape(-1), *([latent_all] * near), latent, gt, si, zero)


def probit_ratio(margin):
    density = jnp.exp(-0.5 * margin * margin - 0.5 * math.log(2.0 * math.pi))
    mass = 0.5 * lax.erfc(-margin / math.sqrt(2.0))
    return density / mass


def body(latent, coords, labels, owner, slot):
    block_count, field_count, point_count = latent.shape
    near_count = owner.shape[1]
    axes = ("blk", "nb")
    device_count = lax.axis_size("blk") * lax.axis_size("nb")
    capacity = max(2, 2 * block_count * near_count // device_count)
    nbr = owner * block_count + slot
    coords_all = lax.all_gather(coords, axes, axis=0, tiled=True)
    latent_all = lax.all_gather(latent, axes, axis=0, tiled=True)
    wanted = owner.reshape(-1)
    places = slot.reshape(-1)
    request_count = wanted.shape[0]
    earlier = lax.broadcasted_iota(
        jnp.int32, (request_count, request_count), 1
    ) < lax.broadcasted_iota(jnp.int32, (request_count, request_count), 0)
    slot_rank = jnp.sum(
        jnp.where((wanted[None, :] == wanted[:, None]) & earlier, 1, 0), axis=1
    ).astype(jnp.int32)
    position = wanted * capacity + slot_rank
    requests = jnp.full((device_count * capacity,), -1, jnp.int32).at[position].set(places)
    kept = lax.all_to_all(
        requests.reshape(device_count, capacity), axes, split_axis=0, concat_axis=0, tiled=True
    )
    gt, si = factor(nbr, coords_all, coords)
    zero = jnp.zeros((device_count * capacity, field_count, point_count), jnp.float32)
    outgoing, own_part = apply_blocks(nbr, position, latent_all, latent, gt, si, zero)
    returned = lax.all_to_all(
        outgoing.reshape(device_count, capacity, field_count, point_count),
        axes, split_axis=0, concat_axis=0, tiled=True,
    )
    asked_flat = kept.reshape(-1)
    selector = (asked_flat[None, :] == lax.broadcasted_iota(jnp.int32, (block_count, 1), 0)).astype(
        jnp.float32
    )
    summed = jnp.dot(
        selector,
        returned.reshape(device_count * capacity, field_count * point_count),
        precision=HI,
        preferred_element_type=jnp.float32,
    )
    prior = summed.reshape(block_count, field_count, point_count) + own_part
    eye = lax.broadcasted_iota(jnp.int32, (128, 128), 0) == lax.broadcasted_iota(jnp.int32, (128, 128), 1)
    qdiag = jnp.sum(jnp.where(eye, si, 0.0), axis=1)
    sign = 2.0 * labels.astype(jnp.float32) - 1.0
    margin = sign * latent
    ratio = probit_ratio(margin)
    weight = ratio * (ratio + margin)
    delta = (sign * ratio - prior) / (weight + qdiag[:, None, :])
    spread = lax.psum(jnp.sum(delta * delta, axis=(0, 2)), axes)
    step_rms = jnp.sqrt(spread / (block_count * point_count * device_count) + 1e-06)
    new_latent = latent + 0.5 * delta / step_rms[None, :, None]
    return (new_latent, step_rms)


def solution(mesh):
    both = ("blk", "nb")
    return jax.shard_map(
        body,
        mesh=mesh,
        in_specs=(P(both, None, None), P(both, None, None), P(both, None, None), P(both, None), P(both, None)),
        out_specs=(P(both, None, None), P()),
        check_vma=False,
    )
```

time: 1860 us -> 565 us (0.30)
  other arithmetic: 1320 us -> 4.32 us
  Pallas kernels: 0 us -> 203 us
  local copies, waits for them, and re-layouts: 130 us -> 43.8 us
  matrix products: 68.2 us -> 8.68 us
  waiting for transfers between devices: 241 us -> 209 us
    another operation x29 -> x0, other arithmetic: 1290 us -> none  [the longest x22 800 us: factor_group(): factor = jnp.linalg.cholesky(covariance(points))]
    pallas_call x0 -> x2, Pallas kernels: none -> 203 us  [the longest x1 176 us: factor(): pl.pallas_call(factor_kernel, out_shape=(jax.ShapeDtypeStruct((n, 128, ne...]
    all_to_all x2 -> x1, waiting for transfers between devices: 166 us -> 0.01 us  [body(): lax.all_to_all(requests.reshape(device_count, capacity), axes, split_axis...]
    all_to_all x1, waiting for transfers between devices: 74.3 us -> 155 us  [body(): lax.all_to_all(outgoing.reshape(device_count, capacity, field_count, poin...]
    another operation x27 -> x0, matrix products: 59.5 us -> none  [the longest x8 33.4 us: factor_group(): factor = jnp.linalg.cholesky(covariance(points))]
    all_gather x0 -> x2, waiting for transfers between devices: none -> 52.6 us  [the longest x1 52.6 us: body(): coords_all = lax.all_gather(coords, axes, axis=0, tiled=True)]
    another operation x22 -> x0, local copies, waits for them, and re-layouts: 30.8 us -> none
    gather x4 -> x0, local copies, waits for them, and re-layouts: 24.2 us -> none  [the longest x2 18.3 us: body(): picked = payload[jnp.maximum(received, 0)]]
  transfers between devices with their start and end apart: 3 -> 4, of which waited for: 3 -> 2; matrix products, arithmetic and copies ran while one was open for 5% -> 2% of each run, Pallas kernels for 0% -> 36%
where the time goes in v1:
time: 565 us; the launch traced here: 564 us
  waiting for transfers between devices  209 us (37%)
  Pallas kernels  203 us (36%)
  blocking collectives  64.1 us (11%)
  local copies, waits for them, and re-layouts  43.8 us (8%)
  starting transfers between devices  17.3 us (3%)
  between operations  14.2 us (3%)
  matrix products  8.68 us (2%)
    pallas_call x1, Pallas kernels, factor(): pl.pallas_call(factor_kernel, out_shape=(jax.ShapeDtypeStruct((n, 128, ne...  176 us
    all_to_all x1, waiting for transfers between devices, body(): lax.all_to_all(outgoing.reshape(device_count, capacity, field_count, poin...  155 us
    psum x1, blocking collectives, body(): spread = lax.psum(jnp.sum(delta * delta, axis=(0, 2)), axes)  64.1 us
    all_gather x1, waiting for transfers between devices, body(): coords_all = lax.all_gather(coords, axes, axis=0, tiled=True)  52.6 us
    pallas_call x1, Pallas kernels, apply_blocks(): pl.pallas_call(apply_kernel, out_shape=(jax.ShapeDtypeStruct(zero.shape,...  26.2 us
    unnamed x15, local copies, waits for them, and re-layouts  22.2 us
    reshape x1, local copies, waits for them, and re-layouts, body(): returned.reshape(device_count * capacity, field_count * point_count)  12.6 us
    all_to_all x1, starting transfers between devices, body(): lax.all_to_all(requests.reshape(device_count, capacity), axes, split_axis...  11.5 us
  transfers between devices with their start and end apart: 4, of which 2 were waited for; matrix products, arithmetic and copies ran while one was open for 2% of the time, Pallas kernels for 36%

profile of v1, /device:TPU:1, one launch (start us, length us, event | category | flops | bytes accessed | tf_op | source)
XLA Modules:
  0.0 564.1 jit_solution(10605689138213934819)
XLA Ops:
  7.2 0.7 all-gather.5.cloned.1.call-update
  7.9 0.0 all-gather.3.cloned.1.call-start
  7.9 0.7 all-gather.3.cloned.1.call-update
  8.6 0.8 copy.31
  9.4 0.8 copy.32
  10.2 0.1 eq.33
  10.2 0.7 broadcast_multiply_fusion
  10.9 0.1 copy.30
  11.0 0.1 mul.65
  11.1 0.1 reshape.65
  11.2 0.2 select_reduce_fusion.1
  11.4 0.7 scatter_custom_fusion
  12.1 0.8 all_to_all.9
  12.8 11.5 %all-to-all-start = ((s32[128,1,2]{2,1,0:T(1,128)}), s32[128,1,2]{2,1,0:T(1,128)S(1)}, u32[]{:S(2)}, u32[]{:S(2)}) async-start(s32[128,1,2]{2,1,0:T(1,128)} %bitcast.2), calls=%async_computation | async-start | bytes 131072 | tf_op jit(solution)/shard_map/all_to_all | solution.py:239
  24.3 0.6 reshape.58.nbr_ref
  24.9 0.5 multiply_add_fusion.1.pos_ref
  25.4 52.6 %all-gather.5.cloned.1.call-done.coords_ref = f32[1024,2,128]{2,1,0:T(2,128)} async-done(((f32[8,2,128]{2,1,0:T(2,128)}), f32[1024,2,128]{2,1,0:T(2,128)}) %all-gather.5.cloned.1.call-update) | async-done | bytes 1048592 | tf_op jit(solution)/shard_map/all_gather | solution.py:226
  78.0 176.3 %factor.1 = (f32[8,128,512]{2,1,0:T(8,128)}, f32[8,128,128]{2,1,0:T(8,128)}) custom-call(s32[8,4]{1,0:T(8,128)} %copy-done.4, s32[8,4]{1,0:T(8,128)} %copy-done.4, f32[1024,2,128]{2,1,0:T(2,128)} %all-gather.5.cloned.1.call-done.coords_ref, f32[8,2,128]{2,1,0:T(2,128)} %own_ref.2), custom_call_target="tpu_custom_call" | custom-call | flops 2000000000 | bytes 5000000 | tf_op jit(solution)/shard_map/factor/pallas_call | solution.py:146
  254.3 6.1 %broadcast_in_dim.28.zero_ref = f32[256,96,128]{2,1,0:T(8,128)} broadcast(f32[]{:T(128)} %constant.15.clone.1), dimensions={} | broadcast | bytes 12582916 | tf_op jit(solution)/shard_map/broadcast_in_dim | solution.py:243
  260.4 26.2 %apply.1 = (f32[256,96,128]{2,1,0:T(8,128)}, f32[8,96,128]{2,1,0:T(8,128)}) custom-call(s32[32]{0:T(128)} %reshape.58.nbr_ref, s32[32]{0:T(128)} %multiply_add_fusion.1.pos_ref, f32[1024,96,128]{2,1,0:T(8,128)} %all-gather.3.cloned.1.call-done.v0_ref.v1_ref.v2_ref.v3_ref, ...), custom_call_target="tpu_custom_call", output_to_operand_aliasing={{0}: (9, {})} | custom-call | tf_op jit(solution)/shard_map/apply/pallas_call | solution.py:191
  286.7 5.8 %all-to-all-start.1 = ((f32[128,2,96,128]{3,2,1,0:T(8,128)}), f32[128,2,96,128]{3,2,1,0:T(8,128)}, u32[]{:S(2)}, u32[]{:S(2)}) async-start(f32[128,2,96,128]{3,2,1,0:T(8,128)} %bitcast.20), calls=%async_computation.1 | async-start | bytes 25165824 | tf_op jit(solution)/shard_map/all_to_all | solution.py:245
  292.5 0.5 broadcast.56
  293.0 0.8 reduce.3
  293.8 0.1 eq.37
  293.9 0.1 select_reduce_fusion
  294.0 155.1 %all-to-all-done.1 = f32[128,2,96,128]{3,2,1,0:T(8,128)} async-done(((f32[128,2,96,128]{3,2,1,0:T(8,128)}), f32[128,2,96,128]{3,2,1,0:T(8,128)}, u32[]{:S(2)}, u32[]{:S(2)}) %all-to-all-start.1) | async-done | bytes 12582944 | tf_op jit(solution)/shard_map/all_to_all | solution.py:245
  449.1 20.6 %copy.46 = f32[32,8,96,128]{3,1,2,0:T(8,128)} copy(f32[32,8,96,128]{3,2,1,0:T(8,128)} %bitcast.9) | data formatting | bytes 25165824
  469.7 12.6 %copy.36 = f32[256,12288]{0,1:T(8,128)} copy(f32[256,12288]{1,0:T(8,128)} %bitcast.22) | data formatting | bytes 25165824 | tf_op jit(solution)/shard_map/reshape | solution.py:255
  482.3 8.7 %fusion.20 = f32[8,96,128]{2,0,1:T(8,128)S(1)} fusion(f32[96,128,256]{2,1,0:T(8,128)} %bitcast.21, s32[256]{0:T(256)S(1)} %eq.37), kind=kOutput, calls=%fused_computation.40 | convolution fusion | flops 301991936 | bytes 12977152 | tf_op jit(solution)/shard_map/dot_general | solution.py:253
  491.0 1.2 multiply_reduce_fusion
  492.2 64.1 %psum.7 = f32[96]{0:T(128)S(1)} all-reduce(f32[96]{0:T(128)S(1)} %get-tuple-element.10), channel_id=1, replica_groups=mesh['blk'=32,'nb'=4] {'blk','nb'}, use_global_device_ids=true, to_apply=%region_4.5 | all-reduce | flops 96 | bytes 768 | tf_op jit(solution)/shard_map/psum | solution.py:267
  556.4 0.9 divide_add_fusion
  (19 shorter events, 0.1 us)
Async XLA Ops:
  7.2 70.8 %all-gather.5.cloned.1.call-start = ((), (), s32[]{:S(2)}) async-start(), calls=%async_computation.3 | async-start | bytes 1056768 | tf_op jit(solution)/shard_map/all_gather | solution.py:226
  7.9 246.4 %all-gather.3.cloned.1.call-start = ((), (), s32[]{:S(2)}) async-start(), calls=%async_computation.2 | async-start | bytes 50724864 | tf_op jit(solution)/shard_map/all_gather | solution.py:227
  12.8 273.8 %all-to-all-start = ((s32[128,1,2]{2,1,0:T(1,128)}), s32[128,1,2]{2,1,0:T(1,128)S(1)}, u32[]{:S(2)}, u32[]{:S(2)}) async-start(s32[128,1,2]{2,1,0:T(1,128)} %bitcast.2), calls=%async_computation | async-start | bytes 131072 | tf_op jit(solution)/shard_map/all_to_all | solution.py:239
  24.3 53.7 %copy-start.4 = (s32[8,4]{1,0:T(8,128)}, s32[8,4]{1,0:T(8,128)S(1)}, u32[]{:S(2)}) copy-start(s32[8,4]{1,0:T(8,128)S(1)} %multiply_add_fusion.nbr_ref.self_ref) | copy-start | bytes 388
  286.6 7.3 %copy-start.1 = (f32[8,128,128]{2,1,0:T(8,128)S(1)}, f32[8,128,128]{2,1,0:T(8,128)}, u32[]{:S(2)}) copy-start(f32[8,128,128]{2,1,0:T(8,128)} %get-tuple-element.7.si_ref) | copy-start | bytes 1572868
  286.7 162.5 %all-to-all-start.1 = ((f32[128,2,96,128]{3,2,1,0:T(8,128)}), f32[128,2,96,128]{3,2,1,0:T(8,128)}, u32[]{:S(2)}, u32[]{:S(2)}) async-start(f32[128,2,96,128]{3,2,1,0:T(8,128)} %bitcast.20), calls=%async_computation.1 | async-start | bytes 25165824 | tf_op jit(solution)/shard_map/all_to_all | solution.py:245
  482.3 8.7 %copy-start = (f32[8,96,128]{2,1,0:T(8,128)S(1)}, f32[8,96,128]{2,1,0:T(8,128)}, u32[]{:S(2)}) copy-start(f32[8,96,128]{2,1,0:T(8,128)} %own_ref.3) | copy-start | bytes 1179652
  482.3 8.7 %copy-start.2 = (s32[8,96,128]{2,1,0:T(8,128)S(1)}, s32[8,96,128]{2,1,0:T(8,128)}, u32[]{:S(2)}) copy-start(s32[8,96,128]{2,1,0:T(8,128)} %param.7) | copy-start | bytes 1179652
  482.3 8.7 %copy-start.3 = (f32[8,96,128]{2,1,0:T(8,128)S(1)}, f32[8,96,128]{2,1,0:T(8,128)}, u32[]{:S(2)}) copy-start(f32[8,96,128]{2,1,0:T(8,128)} %get-tuple-element.9) | copy-start | bytes 1179652
  556.4 0.9 copy-start.5
Sparse Core Ops, SparseCore 0:
  10.8 67.1 all-gather.4
  81.0 132.2 all-gather.2
